TPU v7x, 256 devices: a whole 4x4x8 slice. The times are simulated.
256 devices in a mesh: slab: 16 (over z_hi, x, core), chan: 16 (over y, z_lo).
Axes of the slice: x: 4, y: 4, z: 8 (z_hi: 2, z_lo: 4; z = z_hi * 4 + z_lo), core: 2. Of those that a mesh axis runs over, the one named last changes fastest.
Arguments:
- activations: bfloat16 [2, 128, 32, 16384], P(None, 'chan', 'slab'), may hold values from -6 to 6
- out_grad: bfloat16 [2, 256, 16, 4096], P(None, 'chan', 'slab'), may hold values from -6 to 6
- weights: bfloat16 [27, 128, 256], P(None, 'chan'), may hold values from -0.109375 to 0.109375
Outputs:
- input_grad: bfloat16 [2, 128, 32, 16384], P(None, 'chan', 'slab')
- weight_grad: float32 [27, 128, 256], P(None, 'chan', 'slab')
All inputs are finite; a program needn't handle non-finite values.
Results may differ from a plain program's by a relative error of at most 0.001.
Values may be sent and summed in bfloat16 or wider, within the bound.
A program may use at most 128 MiB of HBM per device.

v0:
```python
import math

import jax
import jax.numpy as jnp
from jax import lax
from jax.sharding import PartitionSpec as P

EDGE = 128


def from_behind(x, axis, by):
    count = lax.axis_size(axis)
    pairs = [(i, i + by) for i in range(count) if 0 <= i + by < count]
    return lax.ppermute(x, axis, pairs)


def flat_back(values, amount):
    zero_part = jnp.zeros(values.shape[:-1] + (amount,), values.dtype)
    return jnp.concatenate([zero_part, values[..., : values.shape[-1] - amount]], axis=-1)


def flat_ahead(values, amount):
    zero_part = jnp.zeros(values.shape[:-1] + (amount,), values.dtype)
    return jnp.concatenate([values[..., amount:], zero_part], axis=-1)


def column_index(length, half_edge):
    return lax.iota(jnp.int32, length) % half_edge


def tap_view(volume, row_tap, col_tap, half_edge):
    cells = half_edge * half_edge
    row_phase = 0 if row_tap == 1 else 1
    col_phase = 0 if col_tap == 1 else 1
    block = row_phase * 2 + col_phase
    picked = volume[..., block * cells : (block + 1) * cells]
    if row_tap == 0:
        picked = flat_back(picked, half_edge)
    if col_tap == 0:
        picked = flat_back(picked, 1)
        keep_mask = column_index(cells, half_edge) != 0
        picked = jnp.where(keep_mask, picked, jnp.zeros_like(picked))
    return picked


def assemble(fetch, half_edge, block_cells):
    last_column = column_index(block_cells, half_edge) == half_edge - 1
    rows_even = [fetch(1, col_tap) for col_tap in range(3)]
    rows_odd = [
        fetch(2, col_tap) + flat_ahead(fetch(0, col_tap), half_edge) for col_tap in range(3)
    ]
    phases = []
    for rows in (rows_even, rows_odd):
        phases.append(rows[1])
        moved = flat_ahead(rows[0], 1)
        phases.append(rows[2] + jnp.where(last_column, jnp.zeros_like(moved), moved))
    return jnp.concatenate(phases, axis=-1)


def body(activations, out_grad, weights):
    samples, chan_local, planes, plane_cells = activations.shape
    half_edge = EDGE // 2
    cells = half_edge * half_edge
    out_planes = planes // 2
    phased = activations.reshape(samples, chan_local, out_planes, 2, plane_cells)
    even_planes = phased[:, :, :, 0]
    odd_planes = phased[:, :, :, 1]
    previous = from_behind(odd_planes[:, :, out_planes - 1], "slab", 1)
    odd_before = jnp.concatenate([previous[:, :, None], odd_planes[:, :, : out_planes - 1]], axis=2)
    depth_views = (odd_before, even_planes, odd_planes)
    following = from_behind(out_grad[:, :, 0], "slab", -1)
    source = jnp.concatenate([out_grad, following[:, :, None]], axis=2)
    signal = lax.all_gather(source, "chan", axis=1, tiled=True)
    own_planes = signal[:, :, :out_planes]
    pieces = []
    for depth_tap in range(3):
        stacked = jnp.stack(
            [
                tap_view(depth_views[depth_tap], row_tap, col_tap, half_edge)
                for row_tap in range(3)
                for col_tap in range(3)
            ]
        )
        pieces.append(
            jnp.einsum("tbcdp,bkdp->tck", stacked, own_planes, preferred_element_type=jnp.float32)
        )
    local_grad = jnp.concatenate(pieces, axis=0)
    total_cells = samples * out_planes * lax.axis_size("slab") * half_edge * half_edge
    weight_grad = lax.psum_scatter(local_grad, "slab", scatter_dimension=2, tiled=True) * (
        1.0 / math.sqrt(total_cells)
    )
    first_block = signal[:, :, 1:]
    blocks = (first_block, own_planes, own_planes)
    folded = []
    for depth_tap in range(3):
        groups = jnp.einsum(
            "tck,bkdp->tbcdp",
            weights[9 * depth_tap : 9 * depth_tap + 9],
            blocks[depth_tap],
            preferred_element_type=jnp.float32,
        )

        def fetch(row_tap, col_tap, groups=groups):
            return groups[3 * row_tap + col_tap]

        folded.append(assemble(fetch, half_edge, cells))
    shifted = folded[0]
    odd_out = folded[2] + shifted
    chan_rows = folded[1].shape[1]
    kept_cells = 4 * cells
    local_grad_in = (
        jnp.stack([folded[1], odd_out], axis=3)
        .reshape(samples, chan_rows, planes, kept_cells)
        .astype(jnp.bfloat16)
    )
    return (local_grad_in, weight_grad)


def solution(mesh):
    placed = (P(None, "chan", "slab", None), P(None, "chan", "slab", None), P(None, "chan", None))
    return jax.shard_map(
        body,
        mesh=mesh,
        in_specs=placed,
        out_specs=(P(None, "chan", "slab", None), P(None, "chan", "slab")),
        check_vma=False,
    )
```

profile of v0, /device:TPU:39, one launch (start us, length us, event | category | flops | bytes accessed | tf_op | source)
XLA Modules:
  0.0 304.0 jit_solution(10184188523158755231)
XLA Ops:
  7.2 2.6 collective-permute-start
  9.8 1.8 copy.115
  11.6 0.1 slice_bitcast_fusion.4
  11.7 9.0 %collective-permute-start.1 = (bf16[2,8,16384]{2,1,0:T(8,128)(2,1)S(1)}, bf16[2,8,16384]{2,1,0:T(8,128)(2,1)S(1)}, u32[]{:S(2)}, u32[]{:S(2)}) collective-permute-start(bf16[2,8,16384]{2,1,0:T(8,128)(2,1)S(1)} %get-tuple-element.32), channel_id=1, source_target_pairs={{0,16},{16,32},{32,48},{48,64},{64,80},{80,96},{96,112},{112,128},... | collective-permute-start | bytes 1572872 | tf_op jit(solution)/shard_map/ppermute | solution.py:14
  21.1 0.1 bitcast_dynamic-update-slice_fusion.14
  21.2 0.1 bitcast_dynamic-update-slice_fusion.13
  21.4 0.1 bitcast_dynamic-update-slice_fusion.11
  21.6 0.8 bitcast_dynamic-update-slice_fusion.10
  22.3 0.9 bitcast_dynamic-update-slice_fusion.8
  23.3 0.8 bitcast_dynamic-update-slice_fusion.7
  24.1 0.8 pad_maximum_fusion.1
  25.0 0.7 bitcast_dynamic-update-slice_fusion.6
  25.7 0.7 fusion.56
  26.4 0.7 fusion.55
  27.1 0.8 bitcast_dynamic-update-slice_fusion.5
  27.9 0.7 fusion.58
  28.5 0.7 fusion.54
  29.2 0.7 fusion.53
  29.9 2.5 collective-permute-done.1
  32.6 0.1 bitcast_dynamic-update-slice_fusion.4
  32.7 0.1 bitcast_dynamic-update-slice_fusion.3
  32.8 0.1 bitcast_dynamic-update-slice_fusion.2
  32.9 0.1 bitcast_dynamic-update-slice_fusion.1
  33.1 0.1 bitcast_dynamic-update-slice_fusion
  33.2 172.3 %all-gather.2.cloned.1.call-done = bf16[2,256,2,4096]{3,1,0,2:T(8,128)(2,1)} async-done(((bf16[2,16,2,4096]{3,1,0,2:T(8,128)(2,1)}), bf16[2,256,2,4096]{3,1,0,2:T(8,128)(2,1)}) %all-gather.2.cloned.1.call-update) | async-done | bytes 8388624 | tf_op jit(solution)/shard_map/all_gather | solution.py:73
  205.6 3.1 %convolution_bitcast_fusion = f32[9,2,8,1,4096]{4,0,2,1,3:T(8,128)S(1)} fusion(bf16[2,256,2,4096]{3,1,0,2:T(8,128)(2,1)} %all-gather.2.cloned.1.call-done, bf16[9,8,256]{2,1,0:T(8,128)(2,1)S(1)} %get-tuple-element.47), kind=kOutput, calls=%fused_computation | convolution fusion | flops 301989888 | bytes 6590464 | tf_op jit(solution)/shard_map/tck,bkdp->tbcdp/dot_general | solution.py:96
  208.6 0.3 slice.336
  208.9 1.0 fusion.72
  210.0 1.5 copy-done.6
  211.5 1.4 fusion.21
  213.0 1.4 fusion.16
  214.4 1.4 fusion.26
  215.8 1.4 copy.59
  217.2 3.0 convolution_bitcast_fusion.2
  220.3 0.1 slice_bitcast_fusion.22
  220.4 0.1 slice.362
  220.5 0.1 slice.359
  220.7 0.1 slice.356
  220.8 0.1 slice.353
  220.9 0.2 copy.114
  221.1 0.2 squeeze.88
  221.3 0.2 copy.117
  221.4 0.1 slice.339
  221.6 0.6 slice.345
  222.2 0.6 slice.342
  222.8 0.6 slice.348
  223.4 3.0 convolution_bitcast_fusion.1
  226.4 0.1 slice_bitcast_fusion.13
  226.6 0.1 slice.377
  226.7 0.1 slice.374
  226.8 0.1 slice.371
  227.0 0.1 slice.368
  227.1 0.2 pad_add_fusion.1
  227.3 0.2 pad_add_fusion
  227.5 0.5 fusion.42
  228.0 0.2 copy.45
  228.3 1.4 pad_add_fusion.2
  229.6 3.2 %fusion.52 = (bf16[2,8,1,4096]{3,2,1,0:T(2,128)(2,1)S(1)}, bf16[2,8,1,4096]{3,2,1,0:T(2,128)(2,1)S(1)}) fusion(f32[9,2,8,1,4096]{4,0,2,1,3:T(8,128)} %copy-done, f32[2,8,1,4032]{3,2,1,0:T(1,128)S(1)} %slice.342, f32[2,8,1,4095]{3,2,1,0:T(1,128)S(1)} %pad_add_fusion.2, pred[4096]{0:T(1024)(128)(4,1)S(1)} %fusion.70, f32[2,8,1,4032]{3,2,1,0:T(1,128)S(1)} %slice.345), kind=kLoop, calls=%fused_computation.84 | loop fusion | flops 393216 | bytes 1568704 | tf_op jit(solution)/shard_map/convert.5
  232.8 1.1 pad_maximum_fusion
  234.0 0.6 copy.116
  234.8 2.1 copy.60
  236.8 58.8 %reduce-scatter.2.cloned.1.call-done = f32[27,8,16]{0,1,2:T(8,128)} async-done(((f32[27,8,256]{0,1,2:T(8,128)}), f32[27,8,16]{0,1,2:T(8,128)}) %reduce-scatter.2.cloned.1.call-update) | async-done | bytes 13840 | tf_op jit(solution)/shard_map/reduce_scatter | solution.py:89
  295.6 0.8 broadcast_multiply_fusion
  296.5 0.6 copy.61
  (41 shorter events, 1.0 us)
Async XLA Ops:
  7.2 198.4 %all-gather.2.cloned.1.call-start = ((), (), s32[]{:S(2)}) async-start(), calls=%async_computation.1 | async-start | bytes 8912896 | tf_op jit(solution)/shard_map/all_gather | solution.py:73
  7.2 16.8 %collective-permute-start = (bf16[2,16,4096]{2,1,0:T(8,128)(2,1)}, bf16[2,16,4096]{2,1,0:T(8,128)(2,1)S(1)}, u32[]{:S(2)}, u32[]{:S(2)}) collective-permute-start(bf16[2,16,4096]{2,1,0:T(8,128)(2,1)} %bitcast.307), channel_id=1, source_target_pairs={{16,0},{32,16},{48,32},{64,48},{80,64},{96,80},{112,96},{128,112},... | collective-permute-start | bytes 786440 | tf_op jit(solution)/shard_map/ppermute | solution.py:14
  11.7 20.7 %collective-permute-start.1 = (bf16[2,8,16384]{2,1,0:T(8,128)(2,1)S(1)}, bf16[2,8,16384]{2,1,0:T(8,128)(2,1)S(1)}, u32[]{:S(2)}, u32[]{:S(2)}) collective-permute-start(bf16[2,8,16384]{2,1,0:T(8,128)(2,1)S(1)} %get-tuple-element.32), channel_id=1, source_target_pairs={{0,16},{16,32},{32,48},{48,64},{64,80},{80,96},{96,112},{112,128},... | collective-permute-start | bytes 1572872 | tf_op jit(solution)/shard_map/ppermute | solution.py:14
  21.2 2.9 copy-start.1
  22.3 1.7 copy-start.3
  24.9 5.0 %copy-start.2 = (bf16[27,8,256]{2,1,0:T(8,128)(2,1)S(1)}, bf16[27,8,256]{2,1,0:T(8,128)(2,1)}, u32[]{:S(2)}) copy-start(bf16[27,8,256]{2,1,0:T(8,128)(2,1)} %param.5) | copy-start | bytes 331780
  24.9 270.7 %reduce-scatter.2.cloned.1.call-start = ((), (), s32[]{:S(2)}) async-start(), calls=%async_computation.2 | async-start | bytes 1114112 | tf_op jit(solution)/shard_map/reduce_scatter | solution.py:89
  205.6 6.0 %copy-start.6 = (bf16[2,256,2,4096]{3,1,0,2:T(8,128)(2,1)S(1)}, bf16[2,256,2,4096]{3,1,0,2:T(8,128)(2,1)}, u32[]{:S(2)}) copy-start(bf16[2,256,2,4096]{3,1,0,2:T(8,128)(2,1)} %all-gather.2.cloned.1.call-done) | copy-start | bytes 25165828
  208.6 4.3 %copy-start = (f32[9,2,8,1,4096]{4,0,2,1,3:T(8,128)}, f32[9,2,8,1,4096]{4,0,2,1,3:T(8,128)S(1)}, u32[]{:S(2)}) copy-start(f32[9,2,8,1,4096]{4,0,2,1,3:T(8,128)S(1)} %convolution_bitcast_fusion) | copy-start | bytes 7077892
  211.5 1.4 copy-start.5
  213.0 1.4 copy-start.4
Sparse Core Ops, SparseCore 0:
  25.0 180.4 all-gather.1
  217.4 78.2 reduce-scatter.1
where the time goes:
time: 309 us; the launch traced here: 304 us
  waiting for transfers between devices  234 us (76%)
  local copies, waits for them, and re-layouts  19.5 us (6%)
  between operations  14.5 us (5%)
  matrix products  13.3 us (4%)
  starting transfers between devices  11.7 us (4%)
  other arithmetic  11.3 us (4%)
    all_gather x1, waiting for transfers between devices, body(): signal = lax.all_gather(source, 'chan', axis=1, tiled=True)  172 us
    reduce_scatter x1, waiting for transfers between devices, body(): lax.psum_scatter(local_grad, 'slab', scatter_dimension=2, tiled=True)  58.8 us
    unnamed x35, local copies, waits for them, and re-layouts  11.8 us
    ppermute x2, starting transfers between devices, from_behind(): return lax.ppermute(x, axis, pairs)  11.6 us
    dot_general x3, matrix products, body(): jnp.einsum('tck,bkdp->tbcdp', weights[9 * depth_tap:9 * depth_tap + 9], b...  9.15 us
  transfers between devices with their start and end apart: 4, of which 3 were waited for; matrix products, arithmetic and copies ran while one was open for 10% of the time, Pallas kernels for 0%

commit v1 on v0

--- a/solution.py
+++ b/solution.py
@@ -1,11 +1,149 @@
+import functools
 import math
 
 import jax
 import jax.numpy as jnp
 from jax import lax
+from jax.experimental import pallas as pl
+from jax.experimental.pallas import tpu as pltpu
 from jax.sharding import PartitionSpec as P
 
 EDGE = 128
+MESH = pl.DeviceIdType.MESH
+ROW = 4
+
+
+def remote(src, dst, send_sem, recv_sem, axis, target):
+    return pltpu.make_async_remote_copy(
+        src_ref=src,
+        dst_ref=dst,
+        send_sem=send_sem,
+        recv_sem=recv_sem,
+        device_id={axis: target},
+        device_id_type=MESH,
+    )
+
+
+def gather_kernel(own_ref, out_ref, local_sem, zs, zr, ys, yr, fs, fr):
+    me = lax.axis_index("chan")
+    y, z = me // ROW, me % ROW
+    rows = own_ref.shape[1]
+
+    def device(y_at, z_at):
+        return ROW * (y_at % ROW) + z_at % ROW
+
+    def slot(index):
+        return pl.ds(pl.multiple_of(index * rows, rows), rows)
+
+    ahead, behind = device(y + 1, z), device(y + ROW - 1, z)
+    z_peers = [device(y, z + k) for k in range(1, ROW)]
+    barrier = pltpu.get_barrier_semaphore()
+    for peer in [ahead, behind] + z_peers:
+        pl.semaphore_signal(barrier, inc=1, device_id={"chan": peer}, device_id_type=MESH)
+    pl.semaphore_wait(barrier, 5)
+
+    sent = []
+
+    def start(copy):
+        copy.start()
+        sent.append(copy)
+        return copy
+
+    mine = out_ref.at[:, slot(me), :]
+    local = pltpu.make_async_copy(own_ref, mine, local_sem)
+
+    def y_send(j):
+        block = device(y, z + ROW - j)
+        place = out_ref.at[:, slot(block), :]
+        source = own_ref if j == 0 else place
+        return [
+            start(remote(source, place, ys.at[2 * j + d], yr.at[2 * j + d], "chan", peer))
+            for d, peer in enumerate((ahead, behind))
+        ]
+
+    def forward(j, copies):
+        result = []
+        for d, peer in enumerate((ahead, behind)):
+            copies[d].wait_recv()
+            block = device(y + (ROW - 1, 1)[d], z + ROW - j)
+            place = out_ref.at[d, slot(block), :]
+            result.append(start(remote(place, place, fs.at[2 * j + d], fr.at[2 * j + d], "chan", peer)))
+        return result
+
+    direct = {0: y_send(0)}
+    along = {}
+    for k in (1, 3, 2):
+        along[k] = start(remote(own_ref, mine, zs.at[k - 1], zr.at[k - 1], "chan", z_peers[k - 1]))
+    local.start()
+    forwarded = forward(0, direct[0])
+    along[1].wait_recv()
+    direct[1] = y_send(1)
+    along[3].wait_recv()
+    direct[3] = y_send(3)
+    forwarded += forward(1, direct[1])
+    along[2].wait_recv()
+    direct[2] = y_send(2)
+    forwarded += forward(3, direct[3])
+    forwarded += forward(2, direct[2])
+    for copy in forwarded:
+        copy.wait_recv()
+    for copy in sent:
+        copy.wait_send()
+    local.wait()
+
+
+def gather(own):
+    samples, rows, cells = own.shape
+    count = ROW * ROW
+    dma = pltpu.SemaphoreType.DMA
+    return pl.pallas_call(
+        gather_kernel,
+        out_shape=jax.ShapeDtypeStruct((samples, rows * count, cells), own.dtype),
+        in_specs=[pl.BlockSpec(memory_space=pltpu.VMEM)],
+        out_specs=pl.BlockSpec(memory_space=pl.ANY),
+        scratch_shapes=[dma, dma((3,)), dma((3,)), dma((8,)), dma((8,)), dma((8,)), dma((8,))],
+        compiler_params=pltpu.CompilerParams(collective_id=0, has_side_effects=True),
+    )(own)
+
+
+def scatter_sum_kernel(scale, parts_ref, out_ref, held, send_sem, recv_sem):
+    count = parts_ref.shape[0]
+    me = lax.axis_index("slab")
+    barrier = pltpu.get_barrier_semaphore()
+    for k in range(1, count):
+        peer = (me + k) % count
+        pl.semaphore_signal(barrier, inc=1, device_id={"slab": peer}, device_id_type=MESH)
+    pl.semaphore_wait(barrier, count - 1)
+    copies = []
+    for k in range(1, count):
+        peer = (me + k) % count
+        copy = remote(parts_ref.at[peer], held.at[k - 1], send_sem.at[k - 1], recv_sem.at[k - 1], "slab", peer)
+        copy.start()
+        copies.append(copy)
+    total = parts_ref[me]
+    for k in range(1, count):
+        copies[k - 1].wait_recv()
+        total += held[k - 1]
+    out_ref[...] = total * scale
+    for copy in copies:
+        copy.wait_send()
+
+
+def scatter_sum(parts, scale):
+    count, rows, lanes = parts.shape
+    dma = pltpu.SemaphoreType.DMA
+    return pl.pallas_call(
+        functools.partial(scatter_sum_kernel, scale),
+        out_shape=jax.ShapeDtypeStruct((rows, lanes), parts.dtype),
+        in_specs=[pl.BlockSpec(memory_space=pltpu.VMEM)],
+        out_specs=pl.BlockSpec(memory_space=pltpu.VMEM),
+        scratch_shapes=[
+            pltpu.VMEM((count - 1, rows, lanes), parts.dtype),
+            dma((count - 1,)),
+            dma((count - 1,)),
+        ],
+        compiler_params=pltpu.CompilerParams(collective_id=1, has_side_effects=True),
+    )(parts)
 
 
 def from_behind(x, axis, by):
@@ -68,10 +206,7 @@
     previous = from_behind(odd_planes[:, :, out_planes - 1], "slab", 1)
     odd_before = jnp.concatenate([previous[:, :, None], odd_planes[:, :, : out_planes - 1]], axis=2)
     depth_views = (odd_before, even_planes, odd_planes)
-    following = from_behind(out_grad[:, :, 0], "slab", -1)
-    source = jnp.concatenate([out_grad, following[:, :, None]], axis=2)
-    signal = lax.all_gather(source, "chan", axis=1, tiled=True)
-    own_planes = signal[:, :, :out_planes]
+    own_planes = gather(out_grad[:, :, 0])[:, :, None]
     pieces = []
     for depth_tap in range(3):
         stacked = jnp.stack(
@@ -85,18 +220,18 @@
             jnp.einsum("tbcdp,bkdp->tck", stacked, own_planes, preferred_element_type=jnp.float32)
         )
     local_grad = jnp.concatenate(pieces, axis=0)
-    total_cells = samples * out_planes * lax.axis_size("slab") * half_edge * half_edge
-    weight_grad = lax.psum_scatter(local_grad, "slab", scatter_dimension=2, tiled=True) * (
-        1.0 / math.sqrt(total_cells)
-    )
-    first_block = signal[:, :, 1:]
-    blocks = (first_block, own_planes, own_planes)
+    count = lax.axis_size("slab")
+    total_cells = samples * out_planes * count * half_edge * half_edge
+    taps, chan_rows, columns = local_grad.shape
+    parts = local_grad.reshape(taps, chan_rows, count, columns // count).transpose(2, 0, 1, 3)
+    parts = parts.reshape(count, taps, chan_rows * columns // count)
+    weight_grad = scatter_sum(parts, 1.0 / math.sqrt(total_cells)).reshape(taps, chan_rows, columns // count)
     folded = []
     for depth_tap in range(3):
         groups = jnp.einsum(
             "tck,bkdp->tbcdp",
             weights[9 * depth_tap : 9 * depth_tap + 9],
-            blocks[depth_tap],
+            own_planes,
             preferred_element_type=jnp.float32,
         )
 
@@ -104,7 +239,7 @@
             return groups[3 * row_tap + col_tap]
 
         folded.append(assemble(fetch, half_edge, cells))
-    shifted = folded[0]
+    shifted = from_behind(folded[0], "slab", -1)
     odd_out = folded[2] + shifted
     chan_rows = folded[1].shape[1]
     kept_cells = 4 * cells

time: 309 us -> 113 us (0.37); the launches traced: 304 us -> 113 us
  waiting for transfers between devices: 234 us -> 0.01 us
  Pallas kernels: 0 us -> 66.1 us
  between operations: 14.5 us -> 1.24 us
  matrix products: 13.3 us -> 8.87 us
    all_gather x1 -> x0, waiting for transfers between devices: 172 us -> none  [body(): signal = lax.all_gather(source, 'chan', axis=1, tiled=True)]
    pallas_call x0 -> x2, Pallas kernels: none -> 66.1 us  [the longest x1 45 us: gather(): pl.pallas_call(gather_kernel, out_shape=jax.ShapeDtypeStruct((samples, ro...]
    reduce_scatter x1 -> x0, waiting for transfers between devices: 58.8 us -> none  [body(): lax.psum_scatter(local_grad, 'slab', scatter_dimension=2, tiled=True)]
    dot_general x3, matrix products: 9.15 us -> 4.63 us  [body(): jnp.einsum('tck,bkdp->tbcdp', weights[9 * depth_tap:9 * depth_tap + 9], o...]
    unnamed x35, local copies, waits for them, and re-layouts: 11.8 us -> 8.62 us
  transfers between devices with their start and end apart: 4 -> 2, of which waited for: 3 -> 0; matrix products, arithmetic and copies ran while one was open for 10% -> 25% of each run, Pallas kernels for 0% -> 59%
where the time goes in v1:
time: 113 us
  Pallas kernels  66.1 us (58%)
  local copies, waits for them, and re-layouts  17.6 us (16%)
  starting transfers between devices  10.5 us (9%)
  matrix products  8.87 us (8%)
  other arithmetic  8.36 us (7%)
  between operations  1.24 us (1%)
    pallas_call x1, Pallas kernels, gather(): pl.pallas_call(gather_kernel, out_shape=jax.ShapeDtypeStruct((samples, ro...  45 us
    pallas_call x1, Pallas kernels, scatter_sum(): pl.pallas_call(functools.partial(scatter_sum_kernel, scale), out_shape=ja...  21.1 us
    ppermute x2, starting transfers between devices, from_behind(): return lax.ppermute(x, axis, pairs)  10.5 us
    unnamed x35, local copies, waits for them, and re-layouts  8.62 us
    dot_general x3, matrix products, body(): jnp.einsum('tck,bkdp->tbcdp', weights[9 * depth_tap:9 * depth_tap + 9], o...  4.63 us
    dot_general x3, matrix products, body(): jnp.einsum('tbcdp,bkdp->tck', stacked, own_planes, preferred_element_type...  4.24 us
    slice x12, local copies, waits for them, and re-layouts, flat_ahead(): return jnp.concatenate([values[..., amount:], zero_part], axis=-1)  2.97 us
    concatenate x2, other arithmetic, assemble(): return jnp.concatenate(phases, axis=-1)  2.41 us
  transfers between devices with their start and end apart: 2, of which 0 were waited for; matrix products, arithmetic and copies ran while one was open for 25% of the time, Pallas kernels for 59%

profile of v1, /device:TPU:39, one launch (start us, length us, event | category | flops | bytes accessed | tf_op | source)
XLA Modules:
  0.0 112.7 jit_solution(6503398751767718565)
XLA Ops:
  0.6 1.8 %copy.118 = bf16[2,8,2,16384]{3,1,0,2:T(8,128)(2,1)S(1)} copy(bf16[2,8,2,16384]{3,2,1,0:T(2,128)(2,1)} %param.3) | data formatting | bytes 2097152 | tf_op args[0]
  2.4 0.1 slice_bitcast_fusion.2
  2.6 8.4 %collective-permute-start.1 = (bf16[2,8,16384]{2,1,0:T(8,128)(2,1)S(1)}, bf16[2,8,16384]{2,1,0:T(8,128)(2,1)S(1)}, u32[]{:S(2)}, u32[]{:S(2)}) collective-permute-start(bf16[2,8,16384]{2,1,0:T(8,128)(2,1)S(1)} %get-tuple-element.32), channel_id=1, source_target_pairs={{0,16},{16,32},{32,48},{48,64},{64,80},{80,96},{96,112},{112,128},... | collective-permute-start | bytes 1572872 | tf_op jit(solution)/shard_map/ppermute | solution.py:152
  11.0 45.0 %shard_map.50 = bf16[2,256,4096]{2,1,0:T(8,128)(2,1)} custom-call(bf16[2,16,4096]{2,1,0:T(8,128)(2,1)} %bitcast.285), custom_call_target="tpu_custom_call" | custom-call | tf_op jit(solution)/shard_map/pallas_call | solution.py:99
  56.1 3.0 %convolution_bitcast_fusion.2 = f32[9,2,8,1,4096]{4,2,1,3,0:T(8,128)S(1)} fusion(bf16[2,256,4096]{2,1,0:T(8,128)(2,1)} %shard_map.50, bf16[9,8,256,1]{2,0,1,3:T(8,128)(2,1)S(1)} %get-tuple-element.57), kind=kOutput, calls=%fused_computation.2 | convolution fusion | flops 301989888 | bytes 6590464 | tf_op jit(solution)/shard_map/tck,bkdp->tbcdp/dot_general | solution.py:231
  59.1 0.8 slice_bitcast_fusion.20
  59.9 0.1 slice.353
  60.1 0.1 slice.350
  60.2 0.1 slice.347
  60.3 0.1 slice.344
  60.5 0.9 copy-done
  61.4 0.8 convolution_bitcast_fusion.1
  62.2 0.7 convolution_bitcast_fusion
  63.0 1.5 %fusion.63 = (f32[1,2,8,1,4096]{4,0,2,1,3:T(1,128)S(1)}, f32[1,2,8,1,4096]{4,0,2,1,3:T(1,128)S(1)}, f32[2,8,1,4096]{3,2,1,0:T(1,128)S(1)}, f32[2,8,1,4096]{3,2,1...) fusion(f32[9,2,8,1,4096]{4,0,2,1,3:T(8,128)S(1)} %convolution_bitcast_fusion), kind=kLoop, calls=%fused_computation.130 | loop fusion | bytes 3145728 | tf_op jit(solution)/shard_map/slice | solution.py:239
  64.4 0.2 copy.120
  64.6 0.1 slice.330
  64.7 0.1 slice_bitcast_fusion.11
  64.9 0.1 slice.367
  65.0 0.1 slice.364
  65.1 0.1 slice.361
  65.3 0.1 slice.358
  65.4 0.2 pad_add_fusion.1
  65.6 0.2 pad_add_fusion
  65.8 1.2 %fusion.40 = (f32[2,8,1,4096]{3,1,0,2:T(8,128)}, f32[2,8,1,4096]{3,1,0,2:T(8,128)}, f32[2,8,1,4096]{3,1,0,2:T(8,128)}, bf16[2,8,1,4096]{3,1,0,2:T(8,128)(2,1)S(1...) fusion(f32[9,2,8,1,4096]{4,2,1,3,0:T(8,128)S(1)} %convolution_bitcast_fusion.2, ...), kind=kLoop, calls=%fused_computation.63 | loop fusion | flops 983040 | bytes 5885632 | tf_op jit(solution)/shard_map/add | solution.py:194
  67.0 1.0 pad_maximum_fusion.1
  68.0 2.1 %collective-permute-start = (f32[2,8,1,16384]{3,1,0,2:T(8,128)}, f32[2,8,1,16384]{3,1,0,2:T(8,128)}, u32[]{:S(2)}, u32[]{:S(2)}) collective-permute-start(f32[2,8,1,16384]{3,1,0,2:T(8,128)} %pad_maximum_fusion.1), channel_id=1, source_target_pairs={{16,0},{32,16},{48,32},{64,48},{80,64},{96,80},{112,96},{128,112},... | collective-permute-start | bytes 3145736 | tf_op jit(solution)/shard_map/ppermute | solution.py:152
  70.3 0.3 slice.327
  70.6 0.1 pad_slice_fusion
  70.7 0.1 pad_slice_fusion.1
  70.8 0.1 bitcast_dynamic-update-slice_fusion.14
  70.9 0.1 bitcast_dynamic-update-slice_fusion.13
  71.0 0.1 bitcast_dynamic-update-slice_fusion.12
  71.1 0.1 bitcast_dynamic-update-slice_fusion.11
  71.3 0.1 bitcast_dynamic-update-slice_fusion.10
  71.4 0.1 bitcast_dynamic-update-slice_fusion.8
  71.5 0.1 bitcast_dynamic-update-slice_fusion.7
  71.6 0.1 bitcast_dynamic-update-slice_fusion.6
  71.8 0.1 bitcast_dynamic-update-slice_fusion.5
  71.9 0.2 copy.117
  72.1 0.2 squeeze.92
  72.3 0.6 slice.336
  72.9 0.6 slice.333
  73.5 0.6 slice.339
  74.1 0.3 copy.44
  74.4 1.2 %pad_add_fusion.2 = f32[2,8,1,4095]{3,2,1,0:T(1,128)S(1)} fusion(f32[2,8,1,4032]{3,2,1,0:T(1,128)S(1)} %slice.339, f32[2,8,1,4096]{3,2,1,0:T(1,128)S(1)} %get-tuple-element.10), kind=kLoop, calls=%fused_computation.65 | loop fusion | flops 65520 | bytes 782208 | tf_op jit(solution)/shard_map/add | solution.py:188
  75.5 0.8 fusion.43
  76.4 1.4 %pad_maximum_fusion = bf16[2,8,1,16384]{3,2,1,0:T(2,128)(2,1)S(1)} fusion(bf16[2,8,1,4096]{3,2,1,0:T(2,128)(2,1)S(1)} %get-tuple-element.13, bf16[2,8,1,4096]{3,2,1,0:T(2,128)(2,1)S(1)} %get-tuple-element.12, bf16[2,8,1,4096]{3,2,1,0:T(2,128)(2,1)S(1)} %copy.44, bf16[2,8,1,4096]{3,2,1,0:T(2,128)(2,1)S(1)} %squeeze.92), kind=kLoop, calls=%fused_computation.18 | loop fusion | flops 2097152 | bytes 1048576 | tf_op jit(solution)/shard_map/concatenate | solution.py:195
  77.8 1.4 %fusion.22 = f32[9,8,256]{2,1,0:T(8,128)S(1)} fusion(bf16[2,256,4096]{2,1,0:T(8,128)(2,1)S(1)} %copy-done, bf16[9,2,8,1,4096]{4,2,1,3,0:T(8,128)(2,1)S(1)} %get-tuple-element.59), kind=kOutput, calls=%fused_computation.17 | convolution fusion | flops 301989888 | bytes 5447680 | tf_op jit(solution)/shard_map/tbcdp,bkdp->tck/dot_general | solution.py:220
  79.2 1.4 %copy.119 = bf16[2,8,1,16384]{3,1,2,0:T(8,128)(2,1)} copy(bf16[2,8,1,16384]{3,2,1,0:T(2,128)(2,1)S(1)} %pad_maximum_fusion) | data formatting | bytes 1048576
  80.6 1.4 %fusion.12 = f32[9,8,256]{2,1,0:T(8,128)S(1)} fusion(bf16[2,256,4096]{2,1,0:T(8,128)(2,1)S(1)} %copy-done, bf16[9,2,8,1,4096]{4,2,1,3,0:T(8,128)(2,1)S(1)} %get-tuple-element.58), kind=kOutput, calls=%fused_computation.15 | convolution fusion | flops 301989888 | bytes 5447680 | tf_op jit(solution)/shard_map/tbcdp,bkdp->tck/dot_general | solution.py:220
  82.0 0.1 pad_slice_fusion.2
  82.1 0.1 bitcast_dynamic-update-slice_fusion.4
  82.3 0.1 bitcast_dynamic-update-slice_fusion.3
  82.4 0.1 bitcast_dynamic-update-slice_fusion.2
  82.5 0.1 bitcast_dynamic-update-slice_fusion.1
  82.6 0.1 bitcast_dynamic-update-slice_fusion
  82.8 1.4 %fusion.17 = f32[9,8,256]{2,1,0:T(8,128)S(1)} fusion(bf16[2,256,4096]{2,1,0:T(8,128)(2,1)S(1)} %copy-done, bf16[9,2,8,1,4096]{4,2,1,0,3:T(8,128)(2,1)S(1)} %fusion.52), kind=kOutput, calls=%fused_computation.16 | convolution fusion | flops 301989888 | bytes 5447680 | tf_op jit(solution)/shard_map/tbcdp,bkdp->tck/dot_general | solution.py:220
  84.2 0.5 reshape.46
  84.7 0.6 copy.70
  85.3 1.2 %reshape.56.parts_ref = f32[16,27,128]{2,1,0:T(8,128)} reshape(f32[16,27,8,16]{3,2,1,0:T(8,128)S(1)} %copy.70) | data formatting | bytes 442368 | tf_op jit(solution)/shard_map/reshape | solution.py:227
  86.6 21.1 %shard_map.51 = f32[27,128]{1,0:T(8,128)} custom-call(f32[16,27,128]{2,1,0:T(8,128)} %reshape.56.parts_ref), custom_call_target="tpu_custom_call" | custom-call | tf_op jit(solution)/shard_map/pallas_call | solution.py:135
  107.7 1.4 %copy.71 = f32[27,128]{0,1:T(8,128)} copy(f32[27,128]{1,0:T(8,128)} %shard_map.51) | data formatting | bytes 27648
  109.2 1.4 %fusion.28 = bf16[2,8,1,1,16384]{4,1,0,3,2:T(8,128)(2,1)S(1)} fusion(f32[2,8,1,16384]{3,1,0,2:T(8,128)} %collective-permute-done, f32[2,8,1,4096]{3,1,0,2:T(8,128)S(1)} %copy-done.4, f32[2,8,1,4096]{3,1,0,2:T(8,128)S(1)} %copy-done.5, f32[2,8,1,4096]{3,1,0,2:T(8,128)S(1)} %copy-done.3, f32[2,8,1,4096]{3,1,0,2:T(8,128)S(1)} %copy-done.2), kind=kLoop, calls=%fused_computation.24 | loop fusion | flops 1310720 | bytes 2621440 | tf_op jit(solution)/shard_map/stack | solution.py:247
  110.7 2.1 %copy.60 = bf16[2,8,2,16384]{3,2,1,0:T(2,128)(2,1)} copy(bf16[2,8,2,16384]{3,1,0,2:T(8,128)(2,1)S(1)} %maximum_bitcast_fusion) | data formatting | bytes 2097152
  (38 shorter events, 0.4 us)
Async XLA Ops:
  2.4 8.5 %copy-start.6 = (bf16[27,8,256]{2,1,0:T(8,128)(2,1)S(1)}, bf16[27,8,256]{2,1,0:T(8,128)(2,1)}, u32[]{:S(2)}) copy-start(bf16[27,8,256]{2,1,0:T(8,128)(2,1)} %param.5) | copy-start | bytes 331780
  2.6 79.4 %collective-permute-start.1 = (bf16[2,8,16384]{2,1,0:T(8,128)(2,1)S(1)}, bf16[2,8,16384]{2,1,0:T(8,128)(2,1)S(1)}, u32[]{:S(2)}, u32[]{:S(2)}) collective-permute-start(bf16[2,8,16384]{2,1,0:T(8,128)(2,1)S(1)} %get-tuple-element.32), channel_id=1, source_target_pairs={{0,16},{16,32},{32,48},{48,64},{64,80},{80,96},{96,112},{112,128},... | collective-permute-start | bytes 1572872 | tf_op jit(solution)/shard_map/ppermute | solution.py:152
  59.1 2.3 %copy-start = (bf16[2,256,4096]{2,1,0:T(8,128)(2,1)S(1)}, bf16[2,256,4096]{2,1,0:T(8,128)(2,1)}, u32[]{:S(2)}) copy-start(bf16[2,256,4096]{2,1,0:T(8,128)(2,1)} %shard_map.50) | copy-start | bytes 12582916
  68.0 41.1 %collective-permute-start = (f32[2,8,1,16384]{3,1,0,2:T(8,128)}, f32[2,8,1,16384]{3,1,0,2:T(8,128)}, u32[]{:S(2)}, u32[]{:S(2)}) collective-permute-start(f32[2,8,1,16384]{3,1,0,2:T(8,128)} %pad_maximum_fusion.1), channel_id=1, source_target_pairs={{16,0},{32,16},{48,32},{64,48},{80,64},{96,80},{112,96},{128,112},... | collective-permute-start | bytes 3145736 | tf_op jit(solution)/shard_map/ppermute | solution.py:152
  85.3 23.8 %copy-start.2 = (f32[2,8,1,4096]{3,1,0,2:T(8,128)S(1)}, f32[2,8,1,4096]{3,1,0,2:T(8,128)}, u32[]{:S(2)}) copy-start(f32[2,8,1,4096]{3,1,0,2:T(8,128)} %get-tuple-element.18) | copy-start | bytes 786436
  85.3 23.8 %copy-start.3 = (f32[2,8,1,4096]{3,1,0,2:T(8,128)S(1)}, f32[2,8,1,4096]{3,1,0,2:T(8,128)}, u32[]{:S(2)}) copy-start(f32[2,8,1,4096]{3,1,0,2:T(8,128)} %get-tuple-element.14) | copy-start | bytes 786436
  85.3 23.8 %copy-start.4 = (f32[2,8,1,4096]{3,1,0,2:T(8,128)S(1)}, f32[2,8,1,4096]{3,1,0,2:T(8,128)}, u32[]{:S(2)}) copy-start(f32[2,8,1,4096]{3,1,0,2:T(8,128)} %get-tuple-element.15) | copy-start | bytes 786436
  85.3 23.8 %copy-start.5 = (f32[2,8,1,4096]{3,1,0,2:T(8,128)S(1)}, f32[2,8,1,4096]{3,1,0,2:T(8,128)}, u32[]{:S(2)}) copy-start(f32[2,8,1,4096]{3,1,0,2:T(8,128)} %get-tuple-element.24) | copy-start | bytes 786436
  109.1 1.4 %copy-start.1 = (bf16[2,8,1,16384]{3,1,2,0:T(8,128)(2,1)S(1)}, bf16[2,8,1,16384]{3,1,2,0:T(8,128)(2,1)}, u32[]{:S(2)}) copy-start(bf16[2,8,1,16384]{3,1,2,0:T(8,128)(2,1)} %copy.119) | copy-start | bytes 1572868
